TPU v7x, 256 devices: a whole 4x4x8 slice. The times are simulated.
256 devices in a mesh: wave: 64 (over z, y, core), field: 4 (over x).
Axes of the slice: x: 4, y: 4, z: 8, core: 2. Of those that a mesh axis runs over, the one named last changes fastest.
Arguments:
- spectra: bfloat16 [640, 2, 160, 640], P('wave', None, 'field'), may hold values from -0.15625 to 0.15625
- legendre: bfloat16 [640, 640, 640], P('wave'), may hold values from -0.25 to 0.25
- block_mask: int32 [640, 10, 10], P('wave'), may hold values from 0 to 1, as said below
- wave_slot: int32 [640], replicated, may hold values from 0 to 639, as said below
- lat_order: int32 [1280], replicated, may hold values from 0 to 1279, each once
- level_order: int32 [160], replicated, may hold values from 0 to 159, each once
Outputs:
- grid_fields: bfloat16 [1280, 160, 3072], P('wave', None, 'field')
Inputs may be any that keep to these rules, and one draw needn't show every extreme that they name: `wave_slot`: each wavenumber from 0 to 639 is held by exactly one slot. `block_mask`: a block is 0 where every total wavenumber of its row block lies below the slot's wavenumber; otherwise it is 0 only in the first few latitude blocks from the pole, fewer than half of them.
All inputs are finite; a program needn't handle non-finite values.
Results may differ from a plain program's by a relative error of at most 0.009.
Values may be sent and summed in bfloat16 or wider, within the bound.
A program may use at most 128 MiB of HBM per device.

v0:
```python
import math
import jax
import jax.numpy as jnp
from jax import lax
from jax.sharding import PartitionSpec as P

BLOCK = 64
NLON = 3072


def spread_mask(block_mask):
    grown = jnp.repeat(jnp.repeat(block_mask, BLOCK, axis=1), BLOCK, axis=2)
    return grown > 0


def fourier_tables(wave_slot, lon_index):
    wavenums = jnp.repeat(wave_slot, 2)
    component = jnp.arange(wavenums.shape[0], dtype=jnp.int32) % 2
    phases = wavenums[:, None] * lon_index[None, :] % NLON
    angles = phases.astype(jnp.float32) * jnp.float32(2.0 * math.pi / NLON)
    weight = jnp.where(wavenums == 0, jnp.float32(1.0), jnp.float32(2.0))[:, None]
    entries = jnp.where(
        component[:, None] == 0, weight * jnp.cos(angles), -weight * jnp.sin(angles)
    )
    high_part = entries.astype(jnp.bfloat16)
    low_part = (entries - high_part.astype(jnp.float32)).astype(jnp.bfloat16)
    slots = wave_slot.shape[0]
    return (
        high_part.reshape(slots, 2, lon_index.shape[0]),
        low_part.reshape(slots, 2, lon_index.shape[0]),
    )


def synthesize(coeff_rows, high_part, low_part):
    from_high = jnp.einsum(
        "stcl,scq->tlq", coeff_rows, high_part, preferred_element_type=jnp.float32
    )
    from_low = jnp.einsum("stcl,scq->tlq", coeff_rows, low_part, preferred_element_type=jnp.float32)
    return (from_high + from_low).astype(jnp.bfloat16)


def shards(spectra, legendre, block_mask, wave_slot, lat_order, level_order):
    slot_count = spectra.shape[0]
    spec_len = spectra.shape[3]
    first_slot = lax.axis_index("wave") * slot_count
    my_waves = lax.dynamic_slice_in_dim(wave_slot, first_slot, slot_count)
    degree = jnp.arange(spec_len, dtype=jnp.int32)
    upper_tri = degree[None, :] >= my_waves[:, None]
    even_deg = (degree[None, :] + my_waves[:, None]) % 2 == 0
    zero_bf = jnp.zeros((), jnp.bfloat16)
    even_spec = jnp.where((upper_tri & even_deg)[:, None, None, :], spectra, zero_bf)
    odd_spec = jnp.where((upper_tri & ~even_deg)[:, None, None, :], spectra, zero_bf)
    kept_poly = jnp.where(spread_mask(block_mask), legendre, zero_bf)
    even_sum = jnp.einsum(
        "snj,scln->sjcl", kept_poly, even_spec, preferred_element_type=jnp.float32
    )
    odd_sum = jnp.einsum("snj,scln->sjcl", kept_poly, odd_spec, preferred_element_type=jnp.float32)
    northern = even_sum + odd_sum
    southern = (even_sum - odd_sum)[:, ::-1]
    coeffs = jnp.concatenate([northern, southern], axis=1).astype(jnp.bfloat16)
    coeffs = jnp.take(coeffs, lat_order, axis=1)
    by_latitude = lax.all_to_all(coeffs, "wave", split_axis=1, concat_axis=0, tiled=True)
    high_part, low_part = fourier_tables(wave_slot, jnp.arange(NLON, dtype=jnp.int32))
    grid_local = synthesize(by_latitude, high_part, low_part)
    columns = lax.all_to_all(grid_local, "field", split_axis=2, concat_axis=1, tiled=True)
    return jnp.take(columns, level_order, axis=1)


def solution(mesh):
    placed = (
        P("wave", None, "field", None),
        P("wave", None, None),
        P("wave", None, None),
        P(),
        P(),
        P(),
    )
    return jax.shard_map(
        shards, mesh=mesh, in_specs=placed, out_specs=P("wave", None, "field"), check_vma=False
    )
```

profile of v0, /device:TPU:1, one launch (start us, length us, event | category | flops | bytes accessed | tf_op | source)
XLA Modules:
  0.0 450.5 jit_solution(13107642925932214233)
XLA Ops:
  0.0 0.7 compare_select_fusion
  0.7 0.7 compare_and_fusion
  1.4 0.8 dynamic_slice.3
  2.2 0.1 fusion.31
  2.3 0.0 copy-start.2
  2.3 12.9 %copy.33 = bf16[10,640,640]{1,2,0:T(8,128)(2,1)} copy(bf16[10,640,640]{2,1,0:T(8,128)(2,1)} %param.7) | data formatting | bytes 16384000 | tf_op args[1]
  15.2 0.0 copy-done.2
  15.2 0.2 copy.32
  15.4 0.3 broadcast_in_dim.80
  15.7 0.3 gt.16
  16.0 0.0 copy-start.1
  16.0 7.6 %bitcast_select_fusion = bf16[10,640,640]{1,2,0:T(8,128)(2,1)} fusion(bf16[10,640,640]{1,2,0:T(8,128)(2,1)} %copy.33, pred[10,640,10]{1,2,0:T(8,128)(4,1)S(1)} %gt.16), kind=kLoop, calls=%fused_computation.3 | loop fusion | flops 4096000 | bytes 16448000 | tf_op jit(solution)/shard_map/jit(_where)/select_n | solution.py:53
  23.6 0.0 copy-start
  23.6 0.0 copy-done.1
  23.6 6.5 %fusion.6 = f32[10,640,2,40]{1,3,2,0:T(8,128)S(1)} fusion(bf16[10,640,640]{1,2,0:T(8,128)(2,1)} %bitcast_select_fusion, bf16[10,2,40,640]{3,2,1,0:T(8,128)(2,1)S(1)} %copy-done.1, pred[10,640]{1,0:T(8,128)(4,1)S(1)} %get-tuple-element.7), kind=kOutput, calls=%fused_computation.15 | convolution fusion | flops 655872000 | bytes 11270400 | tf_op jit(solution)/shard_map/snj,scln->sjcl/dot_general | solution.py:57
  30.1 0.0 copy-done
  30.1 3.0 fusion.44
  33.1 0.3 add_convert_fusion
  33.4 2.5 rev.3
  35.9 1.4 pad_maximum_fusion
  37.3 9.8 %copy.36 = bf16[10,1280,2,40]{3,2,1,0:T(2,128)(2,1)} copy(bf16[10,1280,2,40]{1,3,2,0:T(8,128)(2,1)S(1)} %pad_maximum_fusion) | data formatting | bytes 4096000 | tf_op jit(solution)/shard_map/concatenate | solution.py:60
  47.1 46.7 %gather_fusion = bf16[1280,10,2,40]{3,2,1,0:T(2,128)(2,1)} fusion(bf16[10,1280,2,40]{3,2,1,0:T(2,128)(2,1)} %copy.36, s32[2048]{0:T(1024)S(1)} %pad_clamp_fusion), kind=kCustom, calls=%fused_computation | custom fusion | bytes 4101120 | tf_op jit(solution)/shard_map/jit(_take)/gather | solution.py:61
  93.8 11.2 %fusion.45 = bf16[1280,10,2,40]{3,2,1,0:T(2,128)(2,1)} fusion(bf16[1280,10,2,40]{3,2,1,0:T(2,128)(2,1)} %gather_fusion, pred[1280]{0:T(1024)(128)(4,1)S(1)} %compare_and_fusion), kind=kLoop, calls=%fused_computation.65 | loop fusion | flops 1024000 | bytes 4097280
  105.0 0.0 copy-start.3
  105.0 11.3 %reshape.183 = bf16[64,2,8000]{2,1,0:T(2,128)(2,1)} reshape(bf16[1280,10,2,40]{3,2,1,0:T(2,128)(2,1)} %fusion.45) | data formatting | bytes 4096000
  116.4 13.4 %all-to-all-start = ((bf16[64,2,8000]{2,1,0:T(2,128)(2,1)}), bf16[64,2,8000]{2,1,0:T(2,128)(2,1)S(1)}, u32[]{:S(2)}, u32[]{:S(2)}) async-start(bf16[64,2,8000]{2,1,0:T(2,128)(2,1)} %reshape.183), calls=%async_computation | async-start | bytes 4128768 | tf_op jit(solution)/shard_map/all_to_all | solution.py:62
  129.8 0.0 copy-done.3
  129.9 36.1 %fusion.54 = bf16[640,2,3072,1]{2,0,1,3:T(8,128)(2,1)} fusion(f32[640]{0:T(1024)S(1)} %get-tuple-element.6, s32[640]{0:T(1024)S(1)} %copy-done.3, f32[640]{0:T(1024)S(1)} %get-tuple-element.5, pred[640,2]{0,1:T(4,128)(4,1)S(1)} %fusion.34), kind=kLoop, calls=%fused_computation.22.clone.clone.clone.1 | loop fusion | flops 51118080 | bytes 7873280 | tf_op jit(solution)/shard_map/stcl,scq->tlq/dot_general | solution.py:35
  166.0 36.7 %fusion.56 = bf16[640,2,3072,1]{2,0,1,3:T(8,128)(2,1)} fusion(f32[640]{0:T(1024)S(1)} %get-tuple-element.6, s32[640]{0:T(1024)S(1)} %copy-done.3, f32[640]{0:T(1024)S(1)} %get-tuple-element.5, pred[640,2]{0,1:T(4,128)(4,1)S(1)} %fusion.34), kind=kLoop, calls=%fused_computation.19.clone.clone.1 | loop fusion | flops 62914560 | bytes 7873280 | tf_op jit(solution)/shard_map/stcl,scq->tlq/dot_general | solution.py:38
  202.7 0.0 all-to-all-done
  202.7 8.0 %reshape.184 = bf16[1280,10,2,40]{3,2,1,0:T(2,128)(2,1)} reshape(bf16[64,2,8000]{2,1,0:T(2,128)(2,1)S(1)} %all-to-all-done) | data formatting | bytes 4096000
  210.7 6.8 %copy.38 = bf16[64,10,20,2,40]{4,3,2,1,0:T(2,128)(2,1)} copy(bf16[64,10,20,2,40]{4,3,1,2,0:T(2,128)(2,1)} %bitcast.65) | data formatting | bytes 4096000 | tf_op jit(solution)/shard_map/all_to_all | solution.py:62
  217.5 11.9 %copy.39 = bf16[640,20,2,40]{0,3,2,1:T(8,128)(2,1)S(1)} copy(bf16[640,20,2,40]{3,2,1,0:T(2,128)(2,1)} %bitcast.66) | data formatting | bytes 4096000 | tf_op jit(solution)/shard_map/all_to_all | solution.py:62
  229.5 8.9 %fusion.11 = f32[20,40,3072,1]{2,1,3,0:T(8,128)S(1)} fusion(bf16[640,20,2,40]{0,3,2,1:T(8,128)(2,1)S(1)} %copy.39, bf16[640,2,3072,1]{2,0,1,3:T(8,128)(2,1)} %fusion.56), kind=kOutput, calls=%fused_computation.20 | convolution fusion | flops 6291456000 | bytes 19742720 | tf_op jit(solution)/shard_map/stcl,scq->tlq/dot_general | solution.py:38
  238.3 11.4 %fusion.5 = bf16[20,40,3072]{2,1,0:T(8,128)(2,1)} fusion(f32[20,40,3072,1]{2,1,3,0:T(8,128)S(1)} %fusion.11, bf16[640,20,2,40]{0,3,2,1:T(8,128)(2,1)S(1)} %copy.39, bf16[640,2,3072,1]{2,0,1,3:T(8,128)(2,1)} %fusion.54), kind=kOutput, calls=%fused_computation.14 | convolution fusion | flops 6296371200 | bytes 24657920 | tf_op jit(solution)/shard_map/stcl,scq->tlq/dot_general | solution.py:35
  249.8 19.3 %copy.41 = bf16[20,40,3072]{1,0,2:T(8,128)(2,1)} copy(bf16[20,40,3072]{2,1,0:T(8,128)(2,1)} %fusion.5) | data formatting | bytes 9830400 | tf_op jit(solution)/shard_map/convert_element_type | solution.py:39
  269.1 35.7 %reshape.185 = bf16[4,2,307200]{2,1,0:T(2,128)(2,1)} reshape(bf16[3072,20,40]{2,1,0:T(8,128)(2,1)} %bitcast.63) | data formatting | bytes 9830400
  304.8 0.0 copy-start.4
  304.8 5.4 %all-to-all-start.1 = ((bf16[4,2,307200]{2,1,0:T(2,128)(2,1)}), bf16[4,2,307200]{2,1,0:T(2,128)(2,1)}, u32[]{:S(2)}, u32[]{:S(2)}) async-start(bf16[4,2,307200]{2,1,0:T(2,128)(2,1)} %reshape.185), calls=%async_computation.1 | async-start | bytes 9830400 | tf_op jit(solution)/shard_map/all_to_all | solution.py:65
  310.2 0.0 copy-done.4
  310.2 56.3 %all-to-all-done.1 = bf16[4,2,307200]{2,1,0:T(2,128)(2,1)} async-done(((bf16[4,2,307200]{2,1,0:T(2,128)(2,1)}), bf16[4,2,307200]{2,1,0:T(2,128)(2,1)}, u32[]{:S(2)}, u32[]{:S(2)}) %all-to-all-start.1) | async-done | bytes 4915232 | tf_op jit(solution)/shard_map/all_to_all | solution.py:65
  366.5 36.9 %reshape.186 = bf16[3072,20,40]{2,1,0:T(8,128)(2,1)} reshape(bf16[4,2,307200]{2,1,0:T(2,128)(2,1)} %all-to-all-done.1) | data formatting | bytes 9830400
  403.4 20.9 %copy.55 = bf16[20,40,4,768]{3,2,1,0:T(4,128)(2,1)} copy(bf16[20,40,4,768]{1,0,3,2:T(8,128)(2,1)} %bitcast.64) | data formatting | bytes 9830400 | tf_op jit(solution)/shard_map/all_to_all | solution.py:65
  424.3 7.7 %copy.56 = bf16[20,4,40,768]{3,0,2,1:T(8,128)(2,1)} copy(bf16[20,4,40,768]{3,1,2,0:T(4,128)(2,1)} %bitcast.68) | data formatting | bytes 9830400 | tf_op jit(solution)/shard_map/all_to_all | solution.py:65
  432.0 11.3 %gather_fusion.1 = bf16[160,20,768]{2,1,0:T(8,128)(2,1)} fusion(bf16[20,160,768]{2,0,1:T(8,128)(2,1)} %bitcast.67, s32[1024]{0:T(1024)S(1)} %pad_clamp_fusion.1), kind=kCustom, calls=%fused_computation.1 | custom fusion | bytes 9831040 | tf_op jit(solution)/shard_map/jit(_take)/gather | solution.py:66
  443.4 3.3 select_bitcast_fusion
  446.6 3.3 copy.45
  (7 shorter events, 0.1 us)
Async XLA Ops:
  2.3 12.9 %copy-start.2 = (s32[10,10,10]{2,1,0:T(8,128)S(1)}, s32[10,10,10]{2,1,0:T(8,128)}, u32[]{:S(2)}) copy-start(s32[10,10,10]{2,1,0:T(8,128)} %param.8) | copy-start | bytes 12004
  16.0 7.6 %copy-start.1 = (bf16[10,2,40,640]{3,2,1,0:T(8,128)(2,1)S(1)}, bf16[10,2,40,640]{3,2,1,0:T(8,128)(2,1)}, u32[]{:S(2)}) copy-start(bf16[10,2,40,640]{3,2,1,0:T(8,128)(2,1)} %param.6) | copy-start | bytes 3072004
  23.6 6.5 %copy-start = (bf16[10,640,640]{1,2,0:T(8,128)(2,1)S(1)}, bf16[10,640,640]{1,2,0:T(8,128)(2,1)}, u32[]{:S(2)}) copy-start(bf16[10,640,640]{1,2,0:T(8,128)(2,1)} %bitcast_select_fusion) | copy-start | bytes 24576004
  105.0 24.8 %copy-start.3 = (s32[640]{0:T(1024)S(1)}, s32[640]{0:T(1024)}, u32[]{:S(2)}) copy-start(s32[640]{0:T(1024)} %param.9) | copy-start | bytes 7684
  116.4 86.3 %all-to-all-start = ((bf16[64,2,8000]{2,1,0:T(2,128)(2,1)}), bf16[64,2,8000]{2,1,0:T(2,128)(2,1)S(1)}, u32[]{:S(2)}, u32[]{:S(2)}) async-start(bf16[64,2,8000]{2,1,0:T(2,128)(2,1)} %reshape.183), calls=%async_computation | async-start | bytes 4128768 | tf_op jit(solution)/shard_map/all_to_all | solution.py:62
  304.8 5.4 %copy-start.4 = (s32[160]{0:T(256)S(1)}, s32[160]{0:T(256)}, u32[]{:S(2)}) copy-start(s32[160]{0:T(256)} %param.11) | copy-start | bytes 1924
  304.8 61.7 %all-to-all-start.1 = ((bf16[4,2,307200]{2,1,0:T(2,128)(2,1)}), bf16[4,2,307200]{2,1,0:T(2,128)(2,1)}, u32[]{:S(2)}, u32[]{:S(2)}) async-start(bf16[4,2,307200]{2,1,0:T(2,128)(2,1)} %reshape.185), calls=%async_computation.1 | async-start | bytes 9830400 | tf_op jit(solution)/shard_map/all_to_all | solution.py:65
where the time goes:
time: 458 us; the launch traced here: 450 us
  local copies, waits for them, and re-layouts  247 us (54%)
  other arithmetic  98.1 us (21%)
  waiting for transfers between devices  56.3 us (12%)
  matrix products  29.8 us (7%)
  starting transfers between devices  18.8 us (4%)
    unnamed x15, local copies, waits for them, and re-layouts  105 us
    all_to_all x1, waiting for transfers between devices, shards(): lax.all_to_all(grid_local, 'field', split_axis=2, concat_axis=1, tiled=True)  56.3 us
    gather x1, local copies, waits for them, and re-layouts, shards(): coeffs = jnp.take(coeffs, lat_order, axis=1)  46.7 us
    dot_general x1, other arithmetic, synthesize(): jnp.einsum('stcl,scq->tlq', coeff_rows, low_part, preferred_element_type=...  36.7 us
    dot_general x1, other arithmetic, synthesize(): jnp.einsum('stcl,scq->tlq', coeff_rows, high_part, preferred_element_type...  36.1 us
    all_to_all x2, local copies, waits for them, and re-layouts, shards(): lax.all_to_all(grid_local, 'field', split_axis=2, concat_axis=1, tiled=True)  28.6 us
    convert_element_type x1, local copies, waits for them, and re-layouts, synthesize(): return (from_high + from_low).astype(jnp.bfloat16)  19.3 us
    all_to_all x2, local copies, waits for them, and re-layouts, shards(): lax.all_to_all(coeffs, 'wave', split_axis=1, concat_axis=0, tiled=True)  18.7 us
  transfers between devices with their start and end apart: 2, of which 1 were waited for; matrix products, arithmetic and copies ran while one was open for 16% of the time, Pallas kernels for 0%

commit v1 on v0

--- a/solution.py
+++ b/solution.py
@@ -6,6 +6,22 @@
 
 BLOCK = 64
 NLON = 3072
+
+
+def pairwise_exchange(x, axis, split, join):
+    ways, here = (lax.axis_size(axis), lax.axis_index(axis))
+    width = x.shape[split] // ways
+    shape = list(x.shape)
+    shape[split] = width
+    height = shape[join]
+    shape[join] = height * ways
+    full = jnp.zeros(shape, x.dtype)
+    for mask in range(ways):
+        part = lax.dynamic_slice_in_dim(x, (here ^ mask) * width, width, axis=split)
+        if mask:
+            part = lax.ppermute(part, axis, [(d, d ^ mask) for d in range(ways)])
+        full = lax.dynamic_update_slice_in_dim(full, part, (here ^ mask) * height, axis=join)
+    return full
 
 
 def spread_mask(block_mask):
@@ -62,7 +78,7 @@
     by_latitude = lax.all_to_all(coeffs, "wave", split_axis=1, concat_axis=0, tiled=True)
     high_part, low_part = fourier_tables(wave_slot, jnp.arange(NLON, dtype=jnp.int32))
     grid_local = synthesize(by_latitude, high_part, low_part)
-    columns = lax.all_to_all(grid_local, "field", split_axis=2, concat_axis=1, tiled=True)
+    columns = pairwise_exchange(grid_local, "field", 2, 1)
     return jnp.take(columns, level_order, axis=1)
 
 

time: 458 us -> 328 us (0.72); the launches traced: 450 us -> 326 us
  local copies, waits for them, and re-layouts: 247 us -> 137 us
  waiting for transfers between devices: 56.3 us -> 46.5 us
    unnamed x15 -> x13, local copies, waits for them, and re-layouts: 105 us -> 32.3 us
    all_to_all x1 -> x0, waiting for transfers between devices: 56.3 us -> none  [shards(): lax.all_to_all(grid_local, 'field', split_axis=2, concat_axis=1, tiled=True)]
    ppermute x0 -> x3, waiting for transfers between devices: none -> 46.5 us  [pairwise_exchange(): part = lax.ppermute(part, axis, [(d, d ^ mask) for d in range(ways)])]
    all_to_all x2 -> x0, local copies, waits for them, and re-layouts: 28.6 us -> none  [shards(): lax.all_to_all(grid_local, 'field', split_axis=2, concat_axis=1, tiled=True)]
    convert_element_type x1 -> x0, local copies, waits for them, and re-layouts: 19.3 us -> none  [synthesize(): return (from_high + from_low).astype(jnp.bfloat16)]
    dynamic_update_slice x0 -> x4, local copies, waits for them, and re-layouts: none -> 6.79 us  [pairwise_exchange(): lax.dynamic_update_slice_in_dim(full, part, (here ^ mask) * height, axis=...]
    all_to_all x1 -> x0, starting transfers between devices: 5.37 us -> none  [shards(): lax.all_to_all(grid_local, 'field', split_axis=2, concat_axis=1, tiled=True)]
  transfers between devices with their start and end apart: 2 -> 4, of which waited for: 1 -> 3; matrix products, arithmetic and copies ran while one was open for 16% -> 25% of each run, Pallas kernels for 0% -> 0%
where the time goes in v1:
time: 328 us; the launch traced here: 326 us
  local copies, waits for them, and re-layouts  137 us (42%)
  other arithmetic  98.1 us (30%)
  waiting for transfers between devices  46.5 us (14%)
  matrix products  27.2 us (8%)
  starting transfers between devices  17 us (5%)
    ppermute x3, waiting for transfers between devices, pairwise_exchange(): part = lax.ppermute(part, axis, [(d, d ^ mask) for d in range(ways)])  46.5 us
    gather x1, local copies, waits for them, and re-layouts, shards(): coeffs = jnp.take(coeffs, lat_order, axis=1)  46.4 us
    dot_general x1, other arithmetic, synthesize(): jnp.einsum('stcl,scq->tlq', coeff_rows, low_part, preferred_element_type=...  36.7 us
    dot_general x1, other arithmetic, synthesize(): jnp.einsum('stcl,scq->tlq', coeff_rows, high_part, preferred_element_type...  36.2 us
    unnamed x13, local copies, waits for them, and re-layouts  32.3 us
    all_to_all x2, local copies, waits for them, and re-layouts, shards(): lax.all_to_all(coeffs, 'wave', split_axis=1, concat_axis=0, tiled=True)  18.7 us
    all_to_all x1, starting transfers between devices, shards(): lax.all_to_all(coeffs, 'wave', split_axis=1, concat_axis=0, tiled=True)  13.2 us
    unnamed x1, other arithmetic  11.2 us
  transfers between devices with their start and end apart: 4, of which 3 were waited for; matrix products, arithmetic and copies ran while one was open for 25% of the time, Pallas kernels for 0%

profile of v1, /device:TPU:1, one launch (start us, length us, event | category | flops | bytes accessed | tf_op | source)
XLA Modules:
  0.0 326.4 jit_solution(17147614925112862890)
XLA Ops:
  0.0 0.7 compare_select_fusion
  0.7 0.7 compare_and_fusion
  1.4 0.8 dynamic_slice.15
  2.2 0.1 fusion.31
  2.3 0.0 copy-start.2
  2.3 12.9 %copy.9 = bf16[10,640,640]{1,2,0:T(8,128)(2,1)} copy(bf16[10,640,640]{2,1,0:T(8,128)(2,1)} %param.7) | data formatting | bytes 16384000 | tf_op args[1]
  15.2 0.0 copy-done.2
  15.2 0.2 copy.8
  15.4 0.3 broadcast_in_dim.84
  15.7 0.3 gt.16
  16.0 0.0 copy-start.1
  16.0 7.6 %bitcast_select_fusion = bf16[10,640,640]{1,2,0:T(8,128)(2,1)} fusion(bf16[10,640,640]{1,2,0:T(8,128)(2,1)} %copy.9, pred[10,640,10]{1,2,0:T(8,128)(4,1)S(1)} %gt.16), kind=kLoop, calls=%fused_computation.3 | loop fusion | flops 4096000 | bytes 16448000 | tf_op jit(solution)/shard_map/jit(_where)/select_n | solution.py:69
  23.6 0.0 copy-done.1
  23.6 6.5 %fusion.6 = f32[10,640,2,40]{1,3,2,0:T(8,128)S(1)} fusion(bf16[10,640,640]{1,2,0:T(8,128)(2,1)} %bitcast_select_fusion, bf16[10,2,40,640]{3,2,1,0:T(8,128)(2,1)S(1)} %copy-done.1, pred[10,640]{1,0:T(8,128)(4,1)S(1)} %get-tuple-element.11), kind=kOutput, calls=%fused_computation.15 | convolution fusion | flops 655872000 | bytes 11270400 | tf_op jit(solution)/shard_map/snj,scln->sjcl/dot_general | solution.py:73
  30.1 0.0 copy-done
  30.1 3.0 fusion.44
  33.1 0.3 add_convert_fusion
  33.4 2.5 rev.3
  35.9 1.4 pad_maximum_fusion
  37.3 9.8 %copy.12 = bf16[10,1280,2,40]{3,2,1,0:T(2,128)(2,1)} copy(bf16[10,1280,2,40]{1,3,2,0:T(8,128)(2,1)S(1)} %pad_maximum_fusion) | data formatting | bytes 4096000 | tf_op jit(solution)/shard_map/concatenate | solution.py:76
  47.1 46.4 %gather_fusion = bf16[1280,10,2,40]{3,2,1,0:T(2,128)(2,1)} fusion(bf16[10,1280,2,40]{3,2,1,0:T(2,128)(2,1)} %copy.12, s32[2048]{0:T(1024)S(1)} %pad_clamp_fusion), kind=kCustom, calls=%fused_computation | custom fusion | bytes 4101120 | tf_op jit(solution)/shard_map/jit(_take)/gather | solution.py:77
  93.5 11.2 %fusion.45 = bf16[1280,10,2,40]{3,2,1,0:T(2,128)(2,1)} fusion(bf16[1280,10,2,40]{3,2,1,0:T(2,128)(2,1)} %gather_fusion, pred[1280]{0:T(1024)(128)(4,1)S(1)} %compare_and_fusion), kind=kLoop, calls=%fused_computation.73 | loop fusion | flops 1024000 | bytes 4097280
  104.7 11.3 %reshape.183 = bf16[64,2,8000]{2,1,0:T(2,128)(2,1)} reshape(bf16[1280,10,2,40]{3,2,1,0:T(2,128)(2,1)} %fusion.45) | data formatting | bytes 4096000
  116.1 13.2 %all-to-all-start = ((bf16[64,2,8000]{2,1,0:T(2,128)(2,1)}), bf16[64,2,8000]{2,1,0:T(2,128)(2,1)S(1)}, u32[]{:S(2)}, u32[]{:S(2)}) async-start(bf16[64,2,8000]{2,1,0:T(2,128)(2,1)} %reshape.183), calls=%async_computation | async-start | bytes 4128768 | tf_op jit(solution)/shard_map/all_to_all | solution.py:78
  129.3 36.2 %fusion.54 = bf16[640,2,3072,1]{2,0,1,3:T(8,128)(2,1)} fusion(f32[640]{0:T(1024)S(1)} %get-tuple-element.10, s32[640]{0:T(1024)S(1)} %copy-done.3, f32[640]{0:T(1024)S(1)} %get-tuple-element.9, pred[640,2]{0,1:T(4,128)(4,1)S(1)} %fusion.34), kind=kLoop, calls=%fused_computation.22.clone.clone.clone.1 | loop fusion | flops 51118080 | bytes 7873280 | tf_op jit(solution)/shard_map/stcl,scq->tlq/dot_general | solution.py:51
  165.4 36.7 %fusion.56 = bf16[640,2,3072,1]{2,0,1,3:T(8,128)(2,1)} fusion(f32[640]{0:T(1024)S(1)} %get-tuple-element.10, s32[640]{0:T(1024)S(1)} %copy-done.3, f32[640]{0:T(1024)S(1)} %get-tuple-element.9, pred[640,2]{0,1:T(4,128)(4,1)S(1)} %fusion.34), kind=kLoop, calls=%fused_computation.19.clone.clone.1 | loop fusion | flops 62914560 | bytes 7873280 | tf_op jit(solution)/shard_map/stcl,scq->tlq/dot_general | solution.py:54
  202.1 0.0 all-to-all-done
  202.1 8.0 %reshape.184 = bf16[1280,10,2,40]{3,2,1,0:T(2,128)(2,1)} reshape(bf16[64,2,8000]{2,1,0:T(2,128)(2,1)S(1)} %all-to-all-done) | data formatting | bytes 4096000
  210.2 6.8 %copy.14 = bf16[64,10,20,2,40]{4,3,2,1,0:T(2,128)(2,1)} copy(bf16[64,10,20,2,40]{4,3,1,2,0:T(2,128)(2,1)} %bitcast.57) | data formatting | bytes 4096000 | tf_op jit(solution)/shard_map/all_to_all | solution.py:78
  217.0 11.9 %copy.15 = bf16[640,20,2,40]{0,3,2,1:T(8,128)(2,1)S(1)} copy(bf16[640,20,2,40]{3,2,1,0:T(2,128)(2,1)} %bitcast.58) | data formatting | bytes 4096000 | tf_op jit(solution)/shard_map/all_to_all | solution.py:78
  228.9 8.9 %fusion.11 = f32[20,40,3072,1]{2,1,3,0:T(8,128)S(1)} fusion(bf16[640,20,2,40]{0,3,2,1:T(8,128)(2,1)S(1)} %copy.15, bf16[640,2,3072,1]{2,0,1,3:T(8,128)(2,1)} %fusion.56), kind=kOutput, calls=%fused_computation.20 | convolution fusion | flops 6291456000 | bytes 19742720 | tf_op jit(solution)/shard_map/stcl,scq->tlq/dot_general | solution.py:54
  237.8 8.9 %fusion.5 = bf16[20,40,3072]{2,1,0:T(8,128)(2,1)S(1)} fusion(f32[20,40,3072,1]{2,1,3,0:T(8,128)S(1)} %fusion.11, bf16[640,20,2,40]{0,3,2,1:T(8,128)(2,1)S(1)} %copy.15, bf16[640,2,3072,1]{2,0,1,3:T(8,128)(2,1)} %fusion.54), kind=kOutput, calls=%fused_computation.14 | convolution fusion | flops 6296371200 | bytes 24657920 | tf_op jit(solution)/shard_map/stcl,scq->tlq/dot_general | solution.py:51
  246.6 0.0 copy-start.4
  246.7 2.0 constant_dynamic-slice_fusion
  248.7 1.2 collective-permute-start
  249.9 2.4 collective-permute-start.1
  252.3 0.2 collective-permute-start.2
  252.5 2.9 broadcast_in_dim.82
  255.5 1.4 copy_dynamic-update-slice_fusion.3
  256.8 20.0 %collective-permute-done = bf16[20,40,768]{2,1,0:T(8,128)(2,1)} collective-permute-done((bf16[20,40,768]{2,1,0:T(8,128)(2,1)}, bf16[20,40,768]{2,1,0:T(8,128)(2,1)}, u32[]{:S(2)}, u32[]{:S(2)}) %collective-permute-start) | collective-permute-done | bytes 1228832 | tf_op jit(solution)/shard_map/ppermute | solution.py:22
  276.9 2.7 copy_dynamic-update-slice_fusion.2
  279.5 25.8 %collective-permute-done.1 = bf16[20,40,768]{2,1,0:T(8,128)(2,1)S(1)} collective-permute-done((bf16[20,40,768]{2,1,0:T(8,128)(2,1)}, bf16[20,40,768]{2,1,0:T(8,128)(2,1)S(1)}, u32[]{:S(2)}, u32[]{:S(2)}) %collective-permute-start.1) | collective-permute-done | bytes 1228832 | tf_op jit(solution)/shard_map/ppermute | solution.py:22
  305.3 1.4 copy_dynamic-update-slice_fusion.1
  306.7 0.7 collective-permute-done.2
  307.4 1.4 copy_dynamic-update-slice_fusion
  308.8 11.1 %gather_fusion.1 = bf16[160,20,768]{2,1,0:T(8,128)(2,1)} fusion(bf16[20,160,768]{2,0,1:T(8,128)(2,1)} %copy_dynamic-update-slice_fusion, s32[1024]{0:T(1024)S(1)} %pad_clamp_fusion.1), kind=kCustom, calls=%fused_computation.1 | custom fusion | bytes 9831040 | tf_op jit(solution)/shard_map/jit(_take)/gather | solution.py:82
  319.8 3.3 %select_bitcast_fusion = bf16[20,160,768]{2,0,1:T(8,128)(2,1)S(1)} fusion(bf16[160,20,768]{2,1,0:T(8,128)(2,1)} %gather_fusion.1, pred[160]{0:T(512)(128)(4,1)S(1)} %compare_and_fusion.1), kind=kLoop, calls=%fused_computation.25 | loop fusion | flops 2457600 | bytes 9830560 | tf_op jit(solution)/shard_map/jit(_take)/select_n | solution.py:82
  323.1 3.3 %copy.21 = bf16[20,160,768]{2,1,0:T(8,128)(2,1)} copy(bf16[20,160,768]{2,0,1:T(8,128)(2,1)S(1)} %select_bitcast_fusion) | data formatting | bytes 9830400 | tf_op jit(solution)/shard_map/jit(_take)/select_n | solution.py:82
  (11 shorter events, 0.1 us)
Async XLA Ops:
  2.3 12.9 %copy-start.2 = (s32[10,10,10]{2,1,0:T(8,128)S(1)}, s32[10,10,10]{2,1,0:T(8,128)}, u32[]{:S(2)}) copy-start(s32[10,10,10]{2,1,0:T(8,128)} %param.8) | copy-start | bytes 12004
  16.0 7.6 %copy-start.1 = (bf16[10,2,40,640]{3,2,1,0:T(8,128)(2,1)S(1)}, bf16[10,2,40,640]{3,2,1,0:T(8,128)(2,1)}, u32[]{:S(2)}) copy-start(bf16[10,2,40,640]{3,2,1,0:T(8,128)(2,1)} %param.6) | copy-start | bytes 3072004
  23.6 6.5 %copy-start = (bf16[10,640,640]{1,2,0:T(8,128)(2,1)S(1)}, bf16[10,640,640]{1,2,0:T(8,128)(2,1)}, u32[]{:S(2)}) copy-start(bf16[10,640,640]{1,2,0:T(8,128)(2,1)} %bitcast_select_fusion) | copy-start | bytes 24576004
  104.7 24.6 %copy-start.3 = (s32[640]{0:T(1024)S(1)}, s32[640]{0:T(1024)}, u32[]{:S(2)}) copy-start(s32[640]{0:T(1024)} %param.9) | copy-start | bytes 7684
  116.1 86.1 %all-to-all-start = ((bf16[64,2,8000]{2,1,0:T(2,128)(2,1)}), bf16[64,2,8000]{2,1,0:T(2,128)(2,1)S(1)}, u32[]{:S(2)}, u32[]{:S(2)}) async-start(bf16[64,2,8000]{2,1,0:T(2,128)(2,1)} %reshape.183), calls=%async_computation | async-start | bytes 4128768 | tf_op jit(solution)/shard_map/all_to_all | solution.py:78
  246.6 5.7 %copy-start.4 = (s32[160]{0:T(256)S(1)}, s32[160]{0:T(256)}, u32[]{:S(2)}) copy-start(s32[160]{0:T(256)} %param.11) | copy-start | bytes 1924
  248.7 28.2 %collective-permute-start = (bf16[20,40,768]{2,1,0:T(8,128)(2,1)}, bf16[20,40,768]{2,1,0:T(8,128)(2,1)}, u32[]{:S(2)}, u32[]{:S(2)}) collective-permute-start(bf16[20,40,768]{2,1,0:T(8,128)(2,1)} %get-tuple-element.7), channel_id=1, source_target_pairs={{0,1},{1,0},{2,3},{3,2},{4,5},{5,4},{6,7},{7,6},{8,9},{9,8},{10,11... | collective-permute-start | bytes 3686408 | tf_op jit(solution)/shard_map/ppermute | solution.py:22
  249.9 55.5 %collective-permute-start.1 = (bf16[20,40,768]{2,1,0:T(8,128)(2,1)}, bf16[20,40,768]{2,1,0:T(8,128)(2,1)S(1)}, u32[]{:S(2)}, u32[]{:S(2)}) collective-permute-start(bf16[20,40,768]{2,1,0:T(8,128)(2,1)} %get-tuple-element.6), channel_id=1, source_target_pairs={{0,2},{1,3},{2,0},{3,1},{4,6},{5,7},{6,4},{7,5},{8,10},{9,11},{10,... | collective-permute-start | bytes 3686408 | tf_op jit(solution)/shard_map/ppermute | solution.py:22
  252.3 55.0 %collective-permute-start.2 = (bf16[20,40,768]{2,1,0:T(8,128)(2,1)}, bf16[20,40,768]{2,1,0:T(8,128)(2,1)S(1)}, u32[]{:S(2)}, u32[]{:S(2)}) collective-permute-start(bf16[20,40,768]{2,1,0:T(8,128)(2,1)} %get-tuple-element.5), channel_id=1, source_target_pairs={{0,3},{1,2},{2,1},{3,0},{4,7},{5,6},{6,5},{7,4},{8,11},{9,10},{10,... | collective-permute-start | bytes 3686408 | tf_op jit(solution)/shard_map/ppermute | solution.py:22
